TPU v7x, 128 devices: a whole 4x4x4 slice. The times are simulated.
128 devices in a mesh: slab: 32 (over y, z, core), tile: 4 (over x).
Axes of the slice: x: 4, y: 4, z: 4, core: 2. Of those that a mesh axis runs over, the one named last changes fastest.
Arguments:
- volume: bfloat16 [16, 256, 128, 128], P(None, 'slab', 'tile'), may hold values from -8 to 8
- first_kernel: bfloat16 [16, 4, 3, 3, 3], replicated, may hold values from -0.625 to 0.625
- second_kernel: bfloat16 [16, 4, 3, 3, 3], replicated, may hold values from -0.625 to 0.625
- density_weight: float32 [16], replicated, may hold values from -4 to 4
- upsample_kernel: bfloat16 [3, 3, 16, 16], replicated, may hold values from -4 to 4
- color_weight: bfloat16 [16, 3], replicated, may hold values from -3 to 3
Outputs:
- rendered: float32 [3, 256, 256], P(None, 'tile')
All inputs are finite; a program needn't handle non-finite values.
Results may differ from a plain program's by a relative error of at most 0.0052.
Values may be sent and summed in bfloat16 or wider, within the bound.
A program may use at most 128 MiB of HBM per device.

v0:
```python
import jax
import jax.numpy as jnp
from jax import lax
from jax.sharding import PartitionSpec as P

GROUPS = 4
row_taps = (((1, 0),), ((0, 1), (2, 0)))


def extended_2(cells, sides, width):
    for axis, dim in sides:
        count = lax.axis_size(axis)
        ends = count - 1
        head = lax.slice_in_dim(cells, 0, width, axis=dim)
        tail = lax.slice_in_dim(cells, cells.shape[dim] - width, cells.shape[dim], axis=dim)
        cells = jnp.concatenate(
            [
                lax.ppermute(tail, axis, [(i, (i + 1) % count) for i in range(ends)]),
                cells,
                lax.ppermute(head, axis, [((i + 1) % count, i) for i in range(ends)]),
            ],
            axis=dim,
        )
    return cells


def entering(value, axis, join, neutral):
    count, mine = (lax.axis_size(axis), lax.axis_index(axis))
    pieces = lax.all_gather(value, axis)
    subtotal = jnp.full_like(value, 0) + jnp.asarray(neutral, value.dtype)

    def lap(position, subtotal):
        longer = join(subtotal, pieces[position])
        return jnp.where(position < mine, longer, subtotal)

    return lax.fori_loop(0, count - 1, lap, subtotal)


def shifted(value, axis, steps):
    count = lax.axis_size(axis)
    initial, last = (max(0, -steps), min(count, count - steps))
    return lax.ppermute(value, axis, [(source, source + steps) for source in range(initial, last)])


def convolve(field, kernel, dilation):
    group_width = kernel.shape[1]
    outputs = []
    for group in range(GROUPS):
        piece = field[group * group_width : (group + 1) * group_width]
        weights = kernel[group * group_width : (group + 1) * group_width]
        outputs.append(
            lax.conv_general_dilated(
                piece[None],
                weights,
                (1, 1, 1),
                "VALID",
                rhs_dilation=(dilation, dilation, dilation),
                dimension_numbers=("NCDHW", "OIDHW", "NCDHW"),
                preferred_element_type=jnp.float32,
            )[0]
        )
    return jnp.concatenate(outputs, axis=0)


def decode(shaded, next_row, upsample_kernel, color_weight):
    height = shaded.shape[1]
    breadth = shaded.shape[2]
    extended = jnp.pad(jnp.concatenate([shaded, next_row], axis=1), ((0, 0), (0, 0), (0, 1)))
    outputs = upsample_kernel.shape[3]
    row_pieces = []
    for row_side in range(2):
        col_pieces = []
        for col_side in range(2):
            summed = jnp.zeros((outputs, height, breadth), jnp.float32)
            for row_tap, row_off in row_taps[row_side]:
                for col_tap, col_off in row_taps[col_side]:
                    window = extended[:, row_off : row_off + height, col_off : col_off + breadth]
                    summed = summed + jnp.einsum(
                        "cij,co->oij",
                        window,
                        upsample_kernel[row_tap, col_tap],
                        preferred_element_type=jnp.float32,
                    )
            col_pieces.append(summed)
        row_pieces.append(jnp.stack(col_pieces, axis=-1))
    stacked = jnp.stack(row_pieces, axis=2)
    spread = stacked.reshape(outputs, 2 * height, 2 * breadth)
    hidden = jax.nn.gelu(spread).astype(jnp.bfloat16)
    return jnp.einsum("cij,co->oij", hidden, color_weight, preferred_element_type=jnp.float32)


def add_terms(earlier, later):
    return earlier + later


def body(volume, first_kernel, second_kernel, density_weight, upsample_kernel, color_weight):
    depth_cells = volume.shape[1]
    slab_count = lax.axis_size("slab")
    slab_index = lax.axis_index("slab")
    padded = extended_2(volume, (("slab", 1), ("tile", 2)), 1)
    padded = jnp.pad(padded, ((0, 0), (0, 0), (0, 0), (1, 1)))
    hidden_field = jax.nn.gelu(convolve(padded, first_kernel, 1)).astype(jnp.bfloat16)
    widened = extended_2(hidden_field, (("slab", 1), ("tile", 2)), 2)
    widened = jnp.pad(widened, ((0, 0), (0, 0), (0, 0), (2, 2)))
    features = convolve(widened, second_kernel, 2)
    logits = jnp.einsum("c,czhw->zhw", density_weight, features, precision=lax.Precision.HIGHEST)
    depth_index = (slab_index * depth_cells + jnp.arange(depth_cells)).astype(jnp.float32)
    spacing = 1.0 + 2.0 * depth_index / (depth_cells * slab_count - 1)
    optical = jax.nn.softplus(logits) * spacing[:, None, None]
    slab_sum = jnp.sum(optical, axis=0)
    ray_total = lax.psum(slab_sum, "slab")
    earlier = entering(slab_sum, "slab", add_terms, jnp.zeros_like(slab_sum))
    local_before = jnp.cumsum(optical, axis=0) - optical
    weights = jnp.exp(-local_before / ray_total) * (1.0 - jnp.exp(-optical / ray_total))
    local_picture = jnp.einsum("zhw,czhw->chw", weights, features, precision=lax.Precision.HIGHEST)
    partial_picture = local_picture * jnp.exp(-earlier / ray_total)[None]
    shaded = lax.psum(partial_picture, "slab").astype(jnp.bfloat16)
    next_row = shifted(shaded[:, :1, :], "tile", -1)
    return decode(shaded, next_row, upsample_kernel, color_weight)


def solution(mesh):
    placed = (P(None, "slab", "tile", None), P(), P(), P(), P(), P())
    return jax.shard_map(
        body, mesh=mesh, in_specs=placed, out_specs=P(None, "tile", None), check_vma=False
    )
```

profile of v0, /device:TPU:0, one launch (start us, length us, event | category | flops | bytes accessed | tf_op | source)
XLA Modules:
  0.0 819.2 jit_solution(3985588351069389037)
XLA Ops:
  13.4 4.3 collective-permute-done.3
  24.9 7.4 copy.213
  33.9 27.1 %broadcast_select_fusion.7 = f32[8,32,8,17,4]{2,4,3,1,0:T(4,128)} fusion(pred[8,17]{0,1:T(8,128)(4,1)S(1)} %copy-done.16, bf16[4,10,34,1,7,2]{4,0,5,2,1,3:T(4,128)(2,1)S(1)} %slice.175, bf16[4,10,34,1,8,17]{4,0,5,2,1,3:T(4,128)(2,1)} %copy.213, bf16[16,4,3,3,3]{0,1,4,3,2:T(4,128)(2,1)S(1)} %copy-done.11), kind=kOutput, calls=%fused_computation.52 | convolution fusion | flops 31460608 | bytes 968648 | tf_op jit(solution)/shard_map/conv_general_dilated | solution.py:52
  61.0 8.3 %copy.215 = f32[8,32,8,17,4]{1,0,4,3,2:T(8,128)S(1)} copy(f32[8,32,8,17,4]{2,4,3,1,0:T(4,128)} %broadcast_select_fusion.7) | data formatting | bytes 1114112 | tf_op jit(solution)/shard_map/conv_general_dilated | solution.py:52
  78.7 7.4 copy.218
  87.6 27.9 %broadcast_select_fusion.6 = f32[8,32,8,17,4]{2,4,3,1,0:T(4,128)} fusion(pred[8,17]{0,1:T(8,128)(4,1)S(1)} %copy-done.16, bf16[4,10,34,1,7,2]{4,0,5,2,1,3:T(4,128)(2,1)S(1)} %slice.178, bf16[4,10,34,1,8,17]{4,0,5,2,1,3:T(4,128)(2,1)} %copy.218, bf16[16,4,3,3,3]{0,1,4,3,2:T(4,128)(2,1)S(1)} %copy-done.12), kind=kOutput, calls=%fused_computation.51 | convolution fusion | flops 31460608 | bytes 968648 | tf_op jit(solution)/shard_map/conv_general_dilated | solution.py:52
  115.5 8.3 %copy.220 = f32[8,32,8,17,4]{1,0,4,3,2:T(8,128)S(1)} copy(f32[8,32,8,17,4]{2,4,3,1,0:T(4,128)} %broadcast_select_fusion.6) | data formatting | bytes 1114112 | tf_op jit(solution)/shard_map/conv_general_dilated | solution.py:52
  131.8 7.4 copy.223
  140.8 27.8 %broadcast_select_fusion.5 = f32[8,32,8,17,4]{2,4,3,1,0:T(4,128)} fusion(pred[8,17]{0,1:T(8,128)(4,1)S(1)} %copy-done.16, bf16[4,10,34,1,7,2]{4,0,5,2,1,3:T(4,128)(2,1)S(1)} %slice.181, bf16[4,10,34,1,8,17]{4,0,5,2,1,3:T(4,128)(2,1)} %copy.223, bf16[16,4,3,3,3]{0,1,4,3,2:T(4,128)(2,1)S(1)} %copy-done.13), kind=kOutput, calls=%fused_computation.50 | convolution fusion | flops 31460608 | bytes 968648 | tf_op jit(solution)/shard_map/conv_general_dilated | solution.py:52
  168.5 8.3 %copy.225 = f32[8,32,8,17,4]{1,0,4,3,2:T(8,128)S(1)} copy(f32[8,32,8,17,4]{2,4,3,1,0:T(4,128)} %broadcast_select_fusion.5) | data formatting | bytes 1114112 | tf_op jit(solution)/shard_map/conv_general_dilated | solution.py:52
  184.7 7.4 copy.228
  193.7 28.2 %broadcast_select_fusion.4 = f32[8,32,8,17,4]{2,4,3,1,0:T(4,128)} fusion(pred[8,17]{0,1:T(8,128)(4,1)S(1)} %copy-done.16, bf16[4,10,34,1,7,2]{4,0,5,2,1,3:T(4,128)(2,1)S(1)} %slice.184, bf16[4,10,34,1,8,17]{4,0,5,2,1,3:T(4,128)(2,1)} %copy.228, bf16[16,4,3,3,3]{0,1,4,3,2:T(4,128)(2,1)S(1)} %copy-done.14), kind=kOutput, calls=%fused_computation.49 | convolution fusion | flops 31460608 | bytes 968648 | tf_op jit(solution)/shard_map/conv_general_dilated | solution.py:52
  221.8 8.3 %copy.230 = f32[8,32,8,17,4]{1,0,4,3,2:T(8,128)S(1)} copy(f32[8,32,8,17,4]{2,4,3,1,0:T(4,128)} %broadcast_select_fusion.4) | data formatting | bytes 1114112 | tf_op jit(solution)/shard_map/conv_general_dilated | solution.py:52
  236.1 4.0 collective-permute-start.4
  251.2 4.3 collective-permute-done.7
  263.0 8.9 %copy.240 = bf16[4,12,36,1,8,17]{4,0,5,2,1,3:T(4,128)(2,1)} copy(bf16[4,12,36,1,8,17]{2,0,5,4,1,3:T(4,128)(2,1)S(1)} %bitcast.216) | data formatting | bytes 940032 | tf_op jit(solution)/shard_map/conv_general_dilated | solution.py:52
  274.4 33.4 %broadcast_select_fusion.3 = f32[8,32,8,17,4]{2,4,3,1,0:T(4,128)} fusion(pred[8,17]{0,1:T(8,128)(4,1)S(1)} %copy-done.16, bf16[4,12,36,1,7,4]{4,0,5,2,1,3:T(4,128)(2,1)S(1)} %slice.191, bf16[4,12,36,1,8,17]{4,0,5,2,1,3:T(4,128)(2,1)} %copy.240, bf16[16,4,3,3,3]{0,1,4,3,2:T(4,128)(2,1)S(1)} %copy-done.15), kind=kOutput, calls=%fused_computation.48 | convolution fusion | flops 31962112 | bytes 1127432 | tf_op jit(solution)/shard_map/conv_general_dilated | solution.py:52
  307.8 8.3 %copy.242 = f32[8,32,8,17,4]{1,0,4,3,2:T(8,128)S(1)} copy(f32[8,32,8,17,4]{2,4,3,1,0:T(4,128)} %broadcast_select_fusion.3) | data formatting | bytes 1114112 | tf_op jit(solution)/shard_map/conv_general_dilated | solution.py:52
  325.1 8.9 %copy.245 = bf16[4,12,36,1,8,17]{4,0,5,2,1,3:T(4,128)(2,1)} copy(bf16[4,12,36,1,8,17]{2,0,5,4,1,3:T(4,128)(2,1)S(1)} %bitcast.217) | data formatting | bytes 940032 | tf_op jit(solution)/shard_map/conv_general_dilated | solution.py:52
  336.5 34.0 %broadcast_select_fusion.2 = f32[8,32,8,17,4]{2,4,3,1,0:T(4,128)} fusion(pred[8,17]{0,1:T(8,128)(4,1)S(1)} %copy-done.16, bf16[4,12,36,1,7,4]{4,0,5,2,1,3:T(4,128)(2,1)S(1)} %slice.194, bf16[4,12,36,1,8,17]{4,0,5,2,1,3:T(4,128)(2,1)} %copy.245, bf16[16,4,3,3,3]{0,1,4,3,2:T(4,128)(2,1)S(1)} %copy-done.15), kind=kOutput, calls=%fused_computation.47 | convolution fusion | flops 31962112 | bytes 1127432 | tf_op jit(solution)/shard_map/conv_general_dilated | solution.py:52
  370.4 8.3 %copy.247 = f32[8,32,8,17,4]{1,0,4,3,2:T(8,128)S(1)} copy(f32[8,32,8,17,4]{2,4,3,1,0:T(4,128)} %broadcast_select_fusion.2) | data formatting | bytes 1114112 | tf_op jit(solution)/shard_map/conv_general_dilated | solution.py:52
  387.7 8.9 %copy.250 = bf16[4,12,36,1,8,17]{4,0,5,2,1,3:T(4,128)(2,1)} copy(bf16[4,12,36,1,8,17]{2,0,5,4,1,3:T(4,128)(2,1)S(1)} %bitcast.218) | data formatting | bytes 940032 | tf_op jit(solution)/shard_map/conv_general_dilated | solution.py:52
  399.1 33.3 %broadcast_select_fusion.1 = f32[8,32,8,17,4]{2,4,3,1,0:T(4,128)} fusion(pred[8,17]{0,1:T(8,128)(4,1)S(1)} %copy-done.16, bf16[4,12,36,1,7,4]{4,0,5,2,1,3:T(4,128)(2,1)S(1)} %slice.197, bf16[4,12,36,1,8,17]{4,0,5,2,1,3:T(4,128)(2,1)} %copy.250, bf16[16,4,3,3,3]{0,1,4,3,2:T(4,128)(2,1)S(1)} %copy-done.15), kind=kOutput, calls=%fused_computation.46 | convolution fusion | flops 31962112 | bytes 1127432 | tf_op jit(solution)/shard_map/conv_general_dilated | solution.py:52
  432.4 8.3 %copy.252 = f32[8,32,8,17,4]{1,0,4,3,2:T(8,128)S(1)} copy(f32[8,32,8,17,4]{2,4,3,1,0:T(4,128)} %broadcast_select_fusion.1) | data formatting | bytes 1114112 | tf_op jit(solution)/shard_map/conv_general_dilated | solution.py:52
  449.7 8.9 %copy.255 = bf16[4,12,36,1,8,17]{4,0,5,2,1,3:T(4,128)(2,1)} copy(bf16[4,12,36,1,8,17]{2,0,5,4,1,3:T(4,128)(2,1)S(1)} %bitcast.215) | data formatting | bytes 940032 | tf_op jit(solution)/shard_map/conv_general_dilated | solution.py:52
  461.1 34.2 %broadcast_select_fusion = f32[8,32,8,17,4]{2,4,3,1,0:T(4,128)} fusion(pred[8,17]{0,1:T(8,128)(4,1)S(1)} %copy-done.16, bf16[4,12,36,1,7,4]{4,0,5,2,1,3:T(4,128)(2,1)S(1)} %slice.200, bf16[4,12,36,1,8,17]{4,0,5,2,1,3:T(4,128)(2,1)} %copy.255, bf16[16,4,3,3,3]{0,1,4,3,2:T(4,128)(2,1)S(1)} %copy-done.15), kind=kOutput, calls=%fused_computation.45 | convolution fusion | flops 31962112 | bytes 1127432 | tf_op jit(solution)/shard_map/conv_general_dilated | solution.py:52
  495.3 8.3 %copy.257 = f32[8,32,8,17,4]{1,0,4,3,2:T(8,128)S(1)} copy(f32[8,32,8,17,4]{2,4,3,1,0:T(4,128)} %broadcast_select_fusion) | data formatting | bytes 1114112 | tf_op jit(solution)/shard_map/conv_general_dilated | solution.py:52
  511.7 31.7 %all-gather = f32[1024,128]{1,0:T(8,128)S(1)} all-gather(f32[32,128]{1,0:T(8,128)S(1)} %fusion.107), channel_id=2, replica_groups=mesh['slab'=32,'tile'=4] {'slab'}, dimensions={0}, use_global_device_ids=true | all-gather | bytes 540672 | tf_op jit(solution)/shard_map/all_gather | solution.py:29
  543.4 126.4 %psum.14 = f32[32,128]{1,0:T(8,128)S(1)} all-reduce(f32[32,128]{1,0:T(8,128)S(1)} %fusion.107), channel_id=1, replica_groups=mesh['slab'=32,'tile'=4] {'slab'}, use_global_device_ids=true, to_apply=%region_2.3 | all-reduce | flops 4096 | bytes 32768 | tf_op jit(solution)/shard_map/psum | solution.py:111
  671.6 125.2 %all-reduce.4 = bf16[16,32,128]{2,0,1:T(8,128)(2,1)S(1)} all-reduce(f32[16,32,128]{2,0,1:T(8,128)S(1)} %fusion.103), channel_id=1, replica_groups=mesh['slab'=32,'tile'=4] {'slab'}, use_global_device_ids=true, to_apply=%region_5.6 | all-reduce | flops 65536 | bytes 393216 | tf_op jit(solution)/shard_map/psum | solution.py:117
  804.4 7.9 copy.271
  812.3 5.3 copy.276
  (160 shorter events, 132.3 us)
Async XLA Ops:
  0.0 817.9 %copy-start = (bf16[16,3]{0,1:T(4,128)(2,1)S(1)}, bf16[16,3]{0,1:T(4,128)(2,1)}, u32[]{:S(2)}) copy-start(bf16[16,3]{0,1:T(4,128)(2,1)} %param.13) | copy-start | bytes 292
  1.0 2.6 collective-permute-start
  2.3 5.5 collective-permute-start.1
  8.0 5.4 collective-permute-start.2
  11.4 6.3 collective-permute-start.3
  24.2 9.7 %copy-start.16 = (pred[8,17]{0,1:T(8,128)(4,1)S(1)}, pred[8,17]{0,1:T(8,128)(4,1)}, u32[]{:S(2)}) copy-start(pred[8,17]{0,1:T(8,128)(4,1)} %constant.100) | copy-start | bytes 412
  24.9 9.0 %copy-start.11 = (bf16[16,4,3,3,3]{0,1,4,3,2:T(4,128)(2,1)S(1)}, bf16[16,4,3,3,3]{0,1,4,3,2:T(4,128)(2,1)}, u32[]{:S(2)}) copy-start(bf16[16,4,3,3,3]{0,1,4,3,2:T(4,128)(2,1)} %param.9) | copy-start | bytes 10372
  78.6 9.0 %copy-start.12 = (bf16[16,4,3,3,3]{0,1,4,3,2:T(4,128)(2,1)S(1)}, bf16[16,4,3,3,3]{0,1,4,3,2:T(4,128)(2,1)}, u32[]{:S(2)}) copy-start(bf16[16,4,3,3,3]{0,1,4,3,2:T(4,128)(2,1)} %param.9) | copy-start | bytes 10372
  131.1 9.7 %copy-start.13 = (bf16[16,4,3,3,3]{0,1,4,3,2:T(4,128)(2,1)S(1)}, bf16[16,4,3,3,3]{0,1,4,3,2:T(4,128)(2,1)}, u32[]{:S(2)}) copy-start(bf16[16,4,3,3,3]{0,1,4,3,2:T(4,128)(2,1)} %param.9) | copy-start | bytes 10372
  176.8 5.0 copy-start.4
  184.0 9.7 %copy-start.14 = (bf16[16,4,3,3,3]{0,1,4,3,2:T(4,128)(2,1)S(1)}, bf16[16,4,3,3,3]{0,1,4,3,2:T(4,128)(2,1)}, u32[]{:S(2)}) copy-start(bf16[16,4,3,3,3]{0,1,4,3,2:T(4,128)(2,1)} %param.9) | copy-start | bytes 10372
  230.1 4.2 copy-start.5
  230.1 4.2 copy-start.6
  236.1 5.4 collective-permute-start.4
  240.2 4.2 collective-permute-start.5
  245.6 5.6 collective-permute-start.6
  249.0 6.5 collective-permute-start.7
  263.0 11.4 %copy-start.15 = (bf16[16,4,3,3,3]{0,1,4,3,2:T(4,128)(2,1)S(1)}, bf16[16,4,3,3,3]{0,1,4,3,2:T(4,128)(2,1)}, u32[]{:S(2)}) copy-start(bf16[16,4,3,3,3]{0,1,4,3,2:T(4,128)(2,1)} %param.10) | copy-start | bytes 10372
  503.6 4.3 copy-start.1
  503.6 4.3 copy-start.2
  503.6 5.6 copy-start.10
  503.6 8.0 copy-start.9
  505.1 164.6 %copy-start.7 = (f32[32,128]{1,0:T(8,128)S(1)}, f32[32,128]{1,0:T(8,128)}, u32[]{:S(2)}) copy-start(f32[32,128]{1,0:T(8,128)} %custom-call) | copy-start | bytes 49156
  505.1 166.1 %copy-start.3 = (f32[4,8,32,128]{3,2,1,0:T(8,128)S(1)}, f32[4,8,32,128]{3,2,1,0:T(8,128)}, u32[]{:S(2)}) copy-start(f32[4,8,32,128]{3,2,1,0:T(8,128)} %copy.260) | copy-start | bytes 1572868
  507.9 289.0 %copy-start.8 = (bf16[3,3,16,16]{3,2,1,0:T(8,128)(2,1)S(1)}, bf16[3,3,16,16]{3,2,1,0:T(8,128)(2,1)}, u32[]{:S(2)}) copy-start(bf16[3,3,16,16]{3,2,1,0:T(8,128)(2,1)} %param.12) | copy-start | bytes 13828
  797.3 5.5 collective-permute-start.8
where the time goes:
time: 830 us; the launch traced here: 819 us
  blocking collectives  283 us (34%)
  matrix products  251 us (30%)
  local copies, waits for them, and re-layouts  235 us (28%)
  waiting for transfers between devices  19.3 us (2%)
  starting transfers between devices  18.6 us (2%)
  other arithmetic  10.4 us (1%)
    conv_general_dilated x8, matrix products, convolve(): lax.conv_general_dilated(piece[None], weights, (1, 1, 1), 'VALID', rhs_di...  246 us
    conv_general_dilated x24, local copies, waits for them, and re-layouts, convolve(): lax.conv_general_dilated(piece[None], weights, (1, 1, 1), 'VALID', rhs_di...  148 us
    psum x1, blocking collectives, body(): ray_total = lax.psum(slab_sum, 'slab')  126 us
    psum x1, blocking collectives, body(): shaded = lax.psum(partial_picture, 'slab').astype(jnp.bfloat16)  125 us
    squeeze x16, local copies, waits for them, and re-layouts, convolve(): lax.conv_general_dilated(piece[None], weights, (1, 1, 1), 'VALID', rhs_di...  38.2 us
    all_gather x1, blocking collectives, entering(): pieces = lax.all_gather(value, axis)  31.7 us
    unnamed x44, local copies, waits for them, and re-layouts  23.1 us
  transfers between devices with their start and end apart: 9, of which 7 were waited for; matrix products, arithmetic and copies ran while one was open for 0% of the time, Pallas kernels for 0%

commit v1 on v0

--- a/solution.py
+++ b/solution.py
@@ -114,7 +114,7 @@
     weights = jnp.exp(-local_before / ray_total) * (1.0 - jnp.exp(-optical / ray_total))
     local_picture = jnp.einsum("zhw,czhw->chw", weights, features, precision=lax.Precision.HIGHEST)
     partial_picture = local_picture * jnp.exp(-earlier / ray_total)[None]
-    shaded = lax.psum(partial_picture, "slab").astype(jnp.bfloat16)
+    shaded = jnp.sum(lax.all_gather(partial_picture, "slab"), axis=0).astype(jnp.bfloat16)
     next_row = shifted(shaded[:, :1, :], "tile", -1)
     return decode(shaded, next_row, upsample_kernel, color_weight)
 

time: 830 us -> 771 us (0.929)
  blocking collectives: 283 us -> 158 us
  waiting for transfers between devices: 19.3 us -> 66.9 us
  between operations: 1 us -> 14.4 us
    psum x1 -> x0, blocking collectives: 125 us -> none  [body(): shaded = lax.psum(partial_picture, 'slab').astype(jnp.bfloat16)]
    all_gather x0 -> x1, waiting for transfers between devices: none -> 47.5 us  [body(): lax.all_gather(partial_picture, 'slab')]
  transfers between devices with their start and end apart: 9 -> 10, of which waited for: 7 -> 8; matrix products, arithmetic and copies ran while one was open for 0% -> 0% of each run, Pallas kernels for 0% -> 0%
where the time goes in v1:
time: 771 us; the launch traced here: 760 us
  matrix products  251 us (33%)
  local copies, waits for them, and re-layouts  235 us (30%)
  blocking collectives  158 us (20%)
  waiting for transfers between devices  66.9 us (9%)
  starting transfers between devices  18.6 us (2%)
  other arithmetic  15.2 us (2%)
  between operations  14.4 us (2%)
    conv_general_dilated x8, matrix products, convolve(): lax.conv_general_dilated(piece[None], weights, (1, 1, 1), 'VALID', rhs_di...  246 us
    conv_general_dilated x24, local copies, waits for them, and re-layouts, convolve(): lax.conv_general_dilated(piece[None], weights, (1, 1, 1), 'VALID', rhs_di...  147 us
    psum x1, blocking collectives, body(): ray_total = lax.psum(slab_sum, 'slab')  126 us
    all_gather x1, waiting for transfers between devices, body(): lax.all_gather(partial_picture, 'slab')  47.5 us
    squeeze x16, local copies, waits for them, and re-layouts, convolve(): lax.conv_general_dilated(piece[None], weights, (1, 1, 1), 'VALID', rhs_di...  38.1 us
    all_gather x1, blocking collectives, entering(): pieces = lax.all_gather(value, axis)  31.7 us
    unnamed x44, local copies, waits for them, and re-layouts  23.1 us
  transfers between devices with their start and end apart: 10, of which 8 were waited for; matrix products, arithmetic and copies ran while one was open for 0% of the time, Pallas kernels for 0%

profile of v1, /device:TPU:0, one launch (start us, length us, event | category | flops | bytes accessed | tf_op | source)
XLA Modules:
  0.0 760.0 jit_solution(7342042444242713308)
XLA Ops:
  20.0 4.3 collective-permute-done.3
  31.4 7.3 copy.215
  40.4 27.2 %broadcast_select_fusion.7 = f32[8,32,8,17,4]{2,4,3,1,0:T(4,128)} fusion(pred[8,17]{0,1:T(8,128)(4,1)S(1)} %copy-done.16, bf16[4,10,34,1,7,2]{4,0,5,2,1,3:T(4,128)(2,1)S(1)} %slice.175, bf16[4,10,34,1,8,17]{4,0,5,2,1,3:T(4,128)(2,1)} %copy.215, bf16[16,4,3,3,3]{0,1,4,3,2:T(4,128)(2,1)S(1)} %copy-done.11), kind=kOutput, calls=%fused_computation.52 | convolution fusion | flops 31460608 | bytes 968648 | tf_op jit(solution)/shard_map/conv_general_dilated | solution.py:52
  67.6 8.3 %copy.217 = f32[8,32,8,17,4]{1,0,4,3,2:T(8,128)S(1)} copy(f32[8,32,8,17,4]{2,4,3,1,0:T(4,128)} %broadcast_select_fusion.7) | data formatting | bytes 1114112 | tf_op jit(solution)/shard_map/conv_general_dilated | solution.py:52
  85.2 7.3 copy.220
  94.2 28.0 %broadcast_select_fusion.6 = f32[8,32,8,17,4]{2,4,3,1,0:T(4,128)} fusion(pred[8,17]{0,1:T(8,128)(4,1)S(1)} %copy-done.16, bf16[4,10,34,1,7,2]{4,0,5,2,1,3:T(4,128)(2,1)S(1)} %slice.178, bf16[4,10,34,1,8,17]{4,0,5,2,1,3:T(4,128)(2,1)} %copy.220, bf16[16,4,3,3,3]{0,1,4,3,2:T(4,128)(2,1)S(1)} %copy-done.12), kind=kOutput, calls=%fused_computation.51 | convolution fusion | flops 31460608 | bytes 968648 | tf_op jit(solution)/shard_map/conv_general_dilated | solution.py:52
  122.2 8.3 %copy.222 = f32[8,32,8,17,4]{1,0,4,3,2:T(8,128)S(1)} copy(f32[8,32,8,17,4]{2,4,3,1,0:T(4,128)} %broadcast_select_fusion.6) | data formatting | bytes 1114112 | tf_op jit(solution)/shard_map/conv_general_dilated | solution.py:52
  138.4 7.3 copy.225
  147.3 27.8 %broadcast_select_fusion.5 = f32[8,32,8,17,4]{2,4,3,1,0:T(4,128)} fusion(pred[8,17]{0,1:T(8,128)(4,1)S(1)} %copy-done.16, bf16[4,10,34,1,7,2]{4,0,5,2,1,3:T(4,128)(2,1)S(1)} %slice.181, bf16[4,10,34,1,8,17]{4,0,5,2,1,3:T(4,128)(2,1)} %copy.225, bf16[16,4,3,3,3]{0,1,4,3,2:T(4,128)(2,1)S(1)} %copy-done.13), kind=kOutput, calls=%fused_computation.50 | convolution fusion | flops 31460608 | bytes 968648 | tf_op jit(solution)/shard_map/conv_general_dilated | solution.py:52
  175.2 8.3 %copy.227 = f32[8,32,8,17,4]{1,0,4,3,2:T(8,128)S(1)} copy(f32[8,32,8,17,4]{2,4,3,1,0:T(4,128)} %broadcast_select_fusion.5) | data formatting | bytes 1114112 | tf_op jit(solution)/shard_map/conv_general_dilated | solution.py:52
  191.4 7.3 copy.230
  200.3 28.2 %broadcast_select_fusion.4 = f32[8,32,8,17,4]{2,4,3,1,0:T(4,128)} fusion(pred[8,17]{0,1:T(8,128)(4,1)S(1)} %copy-done.16, bf16[4,10,34,1,7,2]{4,0,5,2,1,3:T(4,128)(2,1)S(1)} %slice.184, bf16[4,10,34,1,8,17]{4,0,5,2,1,3:T(4,128)(2,1)} %copy.230, bf16[16,4,3,3,3]{0,1,4,3,2:T(4,128)(2,1)S(1)} %copy-done.14), kind=kOutput, calls=%fused_computation.49 | convolution fusion | flops 31460608 | bytes 968648 | tf_op jit(solution)/shard_map/conv_general_dilated | solution.py:52
  228.5 8.3 %copy.232 = f32[8,32,8,17,4]{1,0,4,3,2:T(8,128)S(1)} copy(f32[8,32,8,17,4]{2,4,3,1,0:T(4,128)} %broadcast_select_fusion.4) | data formatting | bytes 1114112 | tf_op jit(solution)/shard_map/conv_general_dilated | solution.py:52
  257.9 4.3 collective-permute-done.7
  269.6 8.8 %copy.242 = bf16[4,12,36,1,8,17]{4,0,5,2,1,3:T(4,128)(2,1)} copy(bf16[4,12,36,1,8,17]{2,0,5,4,1,3:T(4,128)(2,1)S(1)} %bitcast.214) | data formatting | bytes 940032 | tf_op jit(solution)/shard_map/conv_general_dilated | solution.py:52
  281.0 33.4 %broadcast_select_fusion.3 = f32[8,32,8,17,4]{2,4,3,1,0:T(4,128)} fusion(pred[8,17]{0,1:T(8,128)(4,1)S(1)} %copy-done.16, bf16[4,12,36,1,7,4]{4,0,5,2,1,3:T(4,128)(2,1)S(1)} %slice.191, bf16[4,12,36,1,8,17]{4,0,5,2,1,3:T(4,128)(2,1)} %copy.242, bf16[16,4,3,3,3]{0,1,4,3,2:T(4,128)(2,1)S(1)} %copy-done.15), kind=kOutput, calls=%fused_computation.48 | convolution fusion | flops 31962112 | bytes 1127432 | tf_op jit(solution)/shard_map/conv_general_dilated | solution.py:52
  314.5 8.3 %copy.244 = f32[8,32,8,17,4]{1,0,4,3,2:T(8,128)S(1)} copy(f32[8,32,8,17,4]{2,4,3,1,0:T(4,128)} %broadcast_select_fusion.3) | data formatting | bytes 1114112 | tf_op jit(solution)/shard_map/conv_general_dilated | solution.py:52
  331.8 8.8 %copy.247 = bf16[4,12,36,1,8,17]{4,0,5,2,1,3:T(4,128)(2,1)} copy(bf16[4,12,36,1,8,17]{2,0,5,4,1,3:T(4,128)(2,1)S(1)} %bitcast.215) | data formatting | bytes 940032 | tf_op jit(solution)/shard_map/conv_general_dilated | solution.py:52
  343.1 34.0 %broadcast_select_fusion.2 = f32[8,32,8,17,4]{2,4,3,1,0:T(4,128)} fusion(pred[8,17]{0,1:T(8,128)(4,1)S(1)} %copy-done.16, bf16[4,12,36,1,7,4]{4,0,5,2,1,3:T(4,128)(2,1)S(1)} %slice.194, bf16[4,12,36,1,8,17]{4,0,5,2,1,3:T(4,128)(2,1)} %copy.247, bf16[16,4,3,3,3]{0,1,4,3,2:T(4,128)(2,1)S(1)} %copy-done.15), kind=kOutput, calls=%fused_computation.47 | convolution fusion | flops 31962112 | bytes 1127432 | tf_op jit(solution)/shard_map/conv_general_dilated | solution.py:52
  377.2 8.3 %copy.249 = f32[8,32,8,17,4]{1,0,4,3,2:T(8,128)S(1)} copy(f32[8,32,8,17,4]{2,4,3,1,0:T(4,128)} %broadcast_select_fusion.2) | data formatting | bytes 1114112 | tf_op jit(solution)/shard_map/conv_general_dilated | solution.py:52
  394.4 8.8 %copy.252 = bf16[4,12,36,1,8,17]{4,0,5,2,1,3:T(4,128)(2,1)} copy(bf16[4,12,36,1,8,17]{2,0,5,4,1,3:T(4,128)(2,1)S(1)} %bitcast.216) | data formatting | bytes 940032 | tf_op jit(solution)/shard_map/conv_general_dilated | solution.py:52
  405.8 33.3 %broadcast_select_fusion.1 = f32[8,32,8,17,4]{2,4,3,1,0:T(4,128)} fusion(pred[8,17]{0,1:T(8,128)(4,1)S(1)} %copy-done.16, bf16[4,12,36,1,7,4]{4,0,5,2,1,3:T(4,128)(2,1)S(1)} %slice.197, bf16[4,12,36,1,8,17]{4,0,5,2,1,3:T(4,128)(2,1)} %copy.252, bf16[16,4,3,3,3]{0,1,4,3,2:T(4,128)(2,1)S(1)} %copy-done.15), kind=kOutput, calls=%fused_computation.46 | convolution fusion | flops 31962112 | bytes 1127432 | tf_op jit(solution)/shard_map/conv_general_dilated | solution.py:52
  439.1 8.3 %copy.254 = f32[8,32,8,17,4]{1,0,4,3,2:T(8,128)S(1)} copy(f32[8,32,8,17,4]{2,4,3,1,0:T(4,128)} %broadcast_select_fusion.1) | data formatting | bytes 1114112 | tf_op jit(solution)/shard_map/conv_general_dilated | solution.py:52
  456.4 8.8 %copy.257 = bf16[4,12,36,1,8,17]{4,0,5,2,1,3:T(4,128)(2,1)} copy(bf16[4,12,36,1,8,17]{2,0,5,4,1,3:T(4,128)(2,1)S(1)} %bitcast.213) | data formatting | bytes 940032 | tf_op jit(solution)/shard_map/conv_general_dilated | solution.py:52
  467.7 34.3 %broadcast_select_fusion = f32[8,32,8,17,4]{2,4,3,1,0:T(4,128)} fusion(pred[8,17]{0,1:T(8,128)(4,1)S(1)} %copy-done.16, bf16[4,12,36,1,7,4]{4,0,5,2,1,3:T(4,128)(2,1)S(1)} %slice.200, bf16[4,12,36,1,8,17]{4,0,5,2,1,3:T(4,128)(2,1)} %copy.257, bf16[16,4,3,3,3]{0,1,4,3,2:T(4,128)(2,1)S(1)} %copy-done.15), kind=kOutput, calls=%fused_computation.45 | convolution fusion | flops 31962112 | bytes 1127432 | tf_op jit(solution)/shard_map/conv_general_dilated | solution.py:52
  502.0 8.3 %copy.259 = f32[8,32,8,17,4]{1,0,4,3,2:T(8,128)S(1)} copy(f32[8,32,8,17,4]{2,4,3,1,0:T(4,128)} %broadcast_select_fusion) | data formatting | bytes 1114112 | tf_op jit(solution)/shard_map/conv_general_dilated | solution.py:52
  518.4 31.7 %all-gather = f32[1024,128]{1,0:T(8,128)S(1)} all-gather(f32[32,128]{1,0:T(8,128)S(1)} %fusion.106), channel_id=2, replica_groups=mesh['slab'=32,'tile'=4] {'slab'}, dimensions={0}, use_global_device_ids=true | all-gather | bytes 540672 | tf_op jit(solution)/shard_map/all_gather | solution.py:29
  550.1 126.4 %psum.7 = f32[32,128]{1,0:T(8,128)S(1)} all-reduce(f32[32,128]{1,0:T(8,128)S(1)} %fusion.106), channel_id=1, replica_groups=mesh['slab'=32,'tile'=4] {'slab'}, use_global_device_ids=true, to_apply=%region_2.3 | all-reduce | flops 4096 | bytes 32768 | tf_op jit(solution)/shard_map/psum | solution.py:111
  678.9 47.5 %all-gather.4.cloned.1.call-done = f32[512,32,128]{2,1,0:T(8,128)} async-done(((f32[16,32,128]{2,1,0:T(8,128)}), f32[512,32,128]{2,1,0:T(8,128)}) %all-gather.4.cloned.1.call-update) | async-done | bytes 8388624 | tf_op jit(solution)/shard_map/all_gather | solution.py:117
  726.5 4.3 reduce_sum.19
  738.3 8.0 %copy.274 = f32[16,32,2,128,2]{0,4,3,2,1:T(2,128)} copy(f32[16,32,2,128,2]{3,0,1,4,2:T(8,128)S(1)} %pad_maximum_fusion.2) | data formatting | bytes 2097152 | tf_op jit(solution)/shard_map/stack | solution.py:86
  746.3 5.3 copy.279
  (164 shorter events, 136.9 us)
Async XLA Ops:
  6.5 745.4 %copy-start = (bf16[16,3]{0,1:T(4,128)(2,1)S(1)}, bf16[16,3]{0,1:T(4,128)(2,1)}, u32[]{:S(2)}) copy-start(bf16[16,3]{0,1:T(4,128)(2,1)} %param.13) | copy-start | bytes 292
  6.5 719.9 %all-gather.4.cloned.1.call-start = ((), (), s32[]{:S(2)}) async-start(), calls=%async_computation | async-start | bytes 8650752 | tf_op jit(solution)/shard_map/all_gather | solution.py:117
  7.5 2.6 collective-permute-start
  8.8 5.5 collective-permute-start.1
  14.5 5.4 collective-permute-start.2
  17.9 6.3 collective-permute-start.3
  30.7 9.6 %copy-start.16 = (pred[8,17]{0,1:T(8,128)(4,1)S(1)}, pred[8,17]{0,1:T(8,128)(4,1)}, u32[]{:S(2)}) copy-start(pred[8,17]{0,1:T(8,128)(4,1)} %constant.100) | copy-start | bytes 412
  31.4 8.9 %copy-start.11 = (bf16[16,4,3,3,3]{0,1,4,3,2:T(4,128)(2,1)S(1)}, bf16[16,4,3,3,3]{0,1,4,3,2:T(4,128)(2,1)}, u32[]{:S(2)}) copy-start(bf16[16,4,3,3,3]{0,1,4,3,2:T(4,128)(2,1)} %param.9) | copy-start | bytes 10372
  85.2 8.9 %copy-start.12 = (bf16[16,4,3,3,3]{0,1,4,3,2:T(4,128)(2,1)S(1)}, bf16[16,4,3,3,3]{0,1,4,3,2:T(4,128)(2,1)}, u32[]{:S(2)}) copy-start(bf16[16,4,3,3,3]{0,1,4,3,2:T(4,128)(2,1)} %param.9) | copy-start | bytes 10372
  137.7 9.6 %copy-start.13 = (bf16[16,4,3,3,3]{0,1,4,3,2:T(4,128)(2,1)S(1)}, bf16[16,4,3,3,3]{0,1,4,3,2:T(4,128)(2,1)}, u32[]{:S(2)}) copy-start(bf16[16,4,3,3,3]{0,1,4,3,2:T(4,128)(2,1)} %param.9) | copy-start | bytes 10372
  183.4 5.0 copy-start.4
  190.7 9.6 %copy-start.14 = (bf16[16,4,3,3,3]{0,1,4,3,2:T(4,128)(2,1)S(1)}, bf16[16,4,3,3,3]{0,1,4,3,2:T(4,128)(2,1)}, u32[]{:S(2)}) copy-start(bf16[16,4,3,3,3]{0,1,4,3,2:T(4,128)(2,1)} %param.9) | copy-start | bytes 10372
  236.8 4.2 copy-start.5
  236.8 4.2 copy-start.6
  242.8 5.4 collective-permute-start.4
  246.8 4.2 collective-permute-start.5
  252.3 5.6 collective-permute-start.6
  255.7 6.5 collective-permute-start.7
  269.6 11.4 %copy-start.15 = (bf16[16,4,3,3,3]{0,1,4,3,2:T(4,128)(2,1)S(1)}, bf16[16,4,3,3,3]{0,1,4,3,2:T(4,128)(2,1)}, u32[]{:S(2)}) copy-start(bf16[16,4,3,3,3]{0,1,4,3,2:T(4,128)(2,1)} %param.10) | copy-start | bytes 10372
  510.3 4.3 copy-start.1
  510.3 4.3 copy-start.2
  510.3 5.5 copy-start.10
  510.3 8.0 %copy-start.9 = (f32[8]{0:T(128)S(1)}, f32[8]{0:T(128)}, u32[]{:S(2)}) copy-start(f32[8]{0:T(128)} %multiply_add_fusion) | copy-start | bytes 100
  511.8 164.6 %copy-start.7 = (f32[32,128]{1,0:T(8,128)S(1)}, f32[32,128]{1,0:T(8,128)}, u32[]{:S(2)}) copy-start(f32[32,128]{1,0:T(8,128)} %custom-call) | copy-start | bytes 49156
  511.9 166.0 %copy-start.3 = (f32[4,8,32,128]{3,2,1,0:T(8,128)S(1)}, f32[4,8,32,128]{3,2,1,0:T(8,128)}, u32[]{:S(2)}) copy-start(f32[4,8,32,128]{3,2,1,0:T(8,128)} %copy.262) | copy-start | bytes 1572868
  677.9 52.9 %copy-start.8 = (bf16[3,3,16,16]{3,2,1,0:T(8,128)(2,1)S(1)}, bf16[3,3,16,16]{3,2,1,0:T(8,128)(2,1)}, u32[]{:S(2)}) copy-start(bf16[3,3,16,16]{3,2,1,0:T(8,128)(2,1)} %param.12) | copy-start | bytes 13828
  731.2 5.5 collective-permute-start.8
Sparse Core Ops, SparseCore 0:
  679.1 47.3 all-gather.3
